TPU v7x, 512 devices: a whole 4x8x8 slice. The times are simulated.
512 devices in a mesh: section: 8 (over x, core), replica: 64 (over z, y).
Axes of the slice: x: 4, y: 8, z: 8, core: 2. Of those that a mesh axis runs over, the one named last changes fastest.
Arguments:
- pending_section_entries: bfloat16 [8, 128, 14, 14, 512], P('section', 'replica'), may hold values from -40 to 40
- arriving_microsets: bfloat16 [1, 128, 14, 14, 512], P(None, 'replica'), may hold values from -40 to 40
- opening_filter_kernel: bfloat16 [8, 3, 3, 512, 512], P('section'), may hold values from -0.09375 to 0.09375
- closing_filter_kernel: bfloat16 [8, 3, 3, 512, 512], P('section'), may hold values from -0.09375 to 0.09375
- stretch_factors: float32 [8, 2, 512], P('section'), may hold values from 0.5 to 1.5
- shift_terms: float32 [8, 2, 512], P('section'), may hold values from -3 to 3
Outputs:
- produced: bfloat16 [8, 2, 128, 14, 14, 512], P('section', None, 'replica')
All inputs are finite; a program needn't handle non-finite values.
Results may differ from a plain program's by a relative error of at most 0.0084.
Values may be sent and summed in bfloat16 or wider, within the bound.
No kernel may reach another device: no remote copies, remote signals or barrier semaphores. Data moves between devices by JAX's collectives and lax.ppermute only.
A program may use at most 64 MiB of HBM per device.

v0:
```python
import jax
import jax.numpy as jnp
from jax import lax
from jax.sharding import PartitionSpec as P

TICKS = 2


def from_behind(shard, axis, by):
    length = lax.axis_size(axis)
    pairs = [(i, i + by) for i in range(length) if 0 <= i + by < length]
    return lax.ppermute(shard, axis, pairs)


def convolve(maps, kernel):
    return lax.conv_general_dilated(
        maps,
        kernel,
        (1, 1),
        "SAME",
        dimension_numbers=("NHWC", "HWIO", "NHWC"),
        preferred_element_type=jnp.float32,
    )


def batch_statistics(conv_out, replica_total):
    summed = lax.psum(jnp.sum(conv_out, axis=(0, 1, 2)), "replica")
    mean = summed / replica_total
    centred = conv_out - mean
    spread = lax.psum(jnp.sum(centred * centred, axis=(0, 1, 2)), "replica")
    var = spread / replica_total
    return (mean, var)


def coefficients(conv_out, gain, bias, replica_total):
    mean, var = batch_statistics(conv_out, replica_total)
    scale = gain * lax.rsqrt(var + 1e-05)
    return (scale, bias - mean * scale)


def store(conv_out):
    return lax.optimization_barrier(conv_out.astype(jnp.bfloat16))


def normalize(stored, scale, offset):
    return jnp.maximum(stored.astype(jnp.float32) * scale + offset, 0.0).astype(jnp.bfloat16)


def body(
    pending_section_entries,
    arriving_microsets,
    opening_filter_kernel,
    closing_filter_kernel,
    stretch_factors,
    shift_terms,
):
    replica_total = (
        lax.axis_size("replica")
        * pending_section_entries.shape[1]
        * pending_section_entries.shape[2]
        * pending_section_entries.shape[3]
    )
    is_first = lax.axis_index("section") == 0
    first_kernel = opening_filter_kernel[0]
    second_kernel = closing_filter_kernel[0]
    current_feature_map = pending_section_entries[0]
    results = []
    for tick in range(TICKS):
        conv_one = convolve(current_feature_map, first_kernel)
        scale_one, offset_one = coefficients(
            conv_one, stretch_factors[0, 0], shift_terms[0, 0], replica_total
        )
        hidden = normalize(store(conv_one), scale_one, offset_one)
        conv_two = convolve(hidden, second_kernel)
        stored_two = store(conv_two)
        last = tick + 1 == TICKS
        scale_two, offset_two = coefficients(
            conv_two, stretch_factors[0, 1], shift_terms[0, 1], replica_total
        )
        output = normalize(stored_two, scale_two, offset_two)
        if not last:
            moved = from_behind(output, "section", 1)
        results.append(output)
        if not last:
            current_feature_map = jnp.where(is_first, arriving_microsets[tick], moved)
    return jnp.stack(results, axis=0)[None]


def solution(mesh):
    in_specs = (
        P("section", "replica", None, None, None),
        P(None, "replica", None, None, None),
        P("section", None, None, None, None),
        P("section", None, None, None, None),
        P("section", None, None),
        P("section", None, None),
    )
    out_specs = P("section", None, "replica", None, None, None)
    return jax.shard_map(body, mesh=mesh, in_specs=in_specs, out_specs=out_specs, check_vma=False)
```

profile of v0, /device:TPU:10, one launch (start us, length us, event | category | flops | bytes accessed | tf_op | source)
XLA Modules:
  0.0 1161.6 jit_solution(2862424807309763926)
XLA Ops:
  0.0 0.8 fusion.68
  0.8 0.8 fusion.69
  1.5 1.4 pad
  3.2 4.6 select_reduce_fusion.7
  7.8 146.3 %psum.56 = f32[512]{0:T(512)S(1)} all-reduce(f32[512]{0:T(512)S(1)} %get-tuple-element.25), channel_id=1, replica_groups=mesh['section'=8,'replica'=64] {'replica'}, use_global_device_ids=true, to_apply=%region_1.0 | all-reduce | flops 512 | bytes 4096 | tf_op jit(solution)/shard_map/psum | solution.py:27
  154.2 0.2 select_reduce_fusion.6
  154.4 141.9 %psum.57 = f32[512]{0:T(512)S(1)} all-reduce(f32[512]{0:T(512)S(1)} %get-tuple-element.19), channel_id=1, replica_groups=mesh['section'=8,'replica'=64] {'replica'}, use_global_device_ids=true, to_apply=%region_3.0 | all-reduce | flops 512 | bytes 4096 | tf_op jit(solution)/shard_map/psum | solution.py:30
  296.4 0.5 copy.17
  296.9 0.2 reshape.18
  297.4 0.2 reshape.23
  297.8 4.6 select_reduce_fusion.5
  302.4 138.0 %psum.58 = f32[512]{0:T(512)S(1)} all-reduce(f32[512]{0:T(512)S(1)} %get-tuple-element.27), channel_id=1, replica_groups=mesh['section'=8,'replica'=64] {'replica'}, use_global_device_ids=true, to_apply=%region_5.0 | all-reduce | flops 512 | bytes 4096 | tf_op jit(solution)/shard_map/psum | solution.py:27
  440.4 0.2 select_reduce_fusion.4
  440.6 140.0 %psum.59 = f32[512]{0:T(512)S(1)} all-reduce(f32[512]{0:T(512)S(1)} %get-tuple-element.17), channel_id=1, replica_groups=mesh['section'=8,'replica'=64] {'replica'}, use_global_device_ids=true, to_apply=%region_7.0 | all-reduce | flops 512 | bytes 4096 | tf_op jit(solution)/shard_map/psum | solution.py:30
  580.6 0.5 copy.20
  581.1 0.2 reshape.27
  581.5 1.9 collective-permute-start
  583.6 7.7 collective-permute-done
  591.5 0.2 reshape.32
  591.9 4.6 select_reduce_fusion.3
  596.5 138.0 %psum.60 = f32[512]{0:T(512)S(1)} all-reduce(f32[512]{0:T(512)S(1)} %get-tuple-element.29), channel_id=1, replica_groups=mesh['section'=8,'replica'=64] {'replica'}, use_global_device_ids=true, to_apply=%region_9.10 | all-reduce | flops 512 | bytes 4096 | tf_op jit(solution)/shard_map/psum | solution.py:27
  734.5 0.2 select_reduce_fusion.2
  734.7 140.0 %psum.61 = f32[512]{0:T(512)S(1)} all-reduce(f32[512]{0:T(512)S(1)} %get-tuple-element.15), channel_id=1, replica_groups=mesh['section'=8,'replica'=64] {'replica'}, use_global_device_ids=true, to_apply=%region_11.12 | all-reduce | flops 512 | bytes 4096 | tf_op jit(solution)/shard_map/psum | solution.py:30
  874.7 0.5 copy.24
  875.2 0.2 reshape.36
  875.7 0.2 reshape.41
  876.1 4.6 select_reduce_fusion.1
  880.7 138.0 %psum.62 = f32[512]{0:T(512)S(1)} all-reduce(f32[512]{0:T(512)S(1)} %get-tuple-element.31), channel_id=1, replica_groups=mesh['section'=8,'replica'=64] {'replica'}, use_global_device_ids=true, to_apply=%region_13.14 | all-reduce | flops 512 | bytes 4096 | tf_op jit(solution)/shard_map/psum | solution.py:27
  1018.7 0.2 select_reduce_fusion
  1018.9 140.0 %psum.63 = f32[512]{0:T(512)S(1)} all-reduce(f32[512]{0:T(512)S(1)} %get-tuple-element.13), channel_id=1, replica_groups=mesh['section'=8,'replica'=64] {'replica'}, use_global_device_ids=true, to_apply=%region_15.16 | all-reduce | flops 512 | bytes 4096 | tf_op jit(solution)/shard_map/psum | solution.py:30
  1158.9 0.5 copy.27
  1159.9 1.7 copy.28
  (35 shorter events, 2.4 us)
Async XLA Ops:
  0.0 3.2 copy-start.1
  581.1 10.2 copy-start
  581.5 9.8 collective-permute-start
where the time goes:
time: 1160 us
  blocking collectives  1120 us (97%)
  matrix products  18.6 us (2%)
    psum x4, blocking collectives, batch_statistics(): spread = lax.psum(jnp.sum(centred * centred, axis=(0, 1, 2)), 'replica')  562 us
    psum x4, blocking collectives, batch_statistics(): summed = lax.psum(jnp.sum(conv_out, axis=(0, 1, 2)), 'replica')  560 us
  transfers between devices with their start and end apart: 1, of which 1 were waited for; matrix products, arithmetic and copies ran while one was open for 0% of the time, Pallas kernels for 0%

commit v1 on v0

--- a/solution.py
+++ b/solution.py
@@ -2,6 +2,7 @@
 import jax.numpy as jnp
 from jax import lax
 from jax.sharding import PartitionSpec as P
+from jax.lax import all_gather
 
 TICKS = 2
 
@@ -24,7 +25,8 @@
 
 
 def batch_statistics(conv_out, replica_total):
-    summed = lax.psum(jnp.sum(conv_out, axis=(0, 1, 2)), "replica")
+    block_in = jnp.sum(conv_out, axis=(0, 1, 2))
+    summed = jnp.sum(all_gather(block_in, "replica"), axis=0)
     mean = summed / replica_total
     centred = conv_out - mean
     spread = lax.psum(jnp.sum(centred * centred, axis=(0, 1, 2)), "replica")

time: 1160 us -> 797 us (0.69)
  the two profiles are of different devices: /device:TPU:10 before, /device:TPU:4 now
where the time goes in v1:
time: 797 us; the launch traced here: 796 us
  blocking collectives  756 us (95%)
  matrix products  18.6 us (2%)
  local copies, waits for them, and re-layouts  9.11 us (1%)
    psum x4, blocking collectives, batch_statistics(): spread = lax.psum(jnp.sum(centred * centred, axis=(0, 1, 2)), 'replica')  563 us
    all_gather x4, blocking collectives, batch_statistics(): summed = jnp.sum(all_gather(block_in, 'replica'), axis=0)  194 us
    conv_general_dilated x4, matrix products, convolve(): lax.conv_general_dilated(maps, kernel, (1, 1), 'SAME', dimension_numbers=...  18.6 us
  transfers between devices with their start and end apart: 1, of which 1 were waited for; matrix products, arithmetic and copies ran while one was open for 0% of the time, Pallas kernels for 0%

profile of v1, /device:TPU:4, one launch (start us, length us, event | category | flops | bytes accessed | tf_op | source)
XLA Modules:
  0.0 796.1 jit_solution(5633133422505254675)
XLA Ops:
  0.0 0.8 fusion.68
  0.8 0.8 fusion.69
  1.5 1.4 pad
  3.2 4.6 select_reduce_fusion.7
  7.8 56.3 %all-gather.4 = f32[64,1,512]{2,1,0:T(1,128)S(1)} all-gather(f32[1,1,512]{2,1,0:T(1,128)S(1)} %bitcast.98), channel_id=2, replica_groups=mesh['section'=8,'replica'=64] {'replica'}, dimensions={0}, use_global_device_ids=true | all-gather | bytes 133120 | tf_op jit(solution)/shard_map/all_gather | solution.py:29
  64.3 0.2 select_reduce_fusion.6
  64.5 140.6 %psum.28 = f32[512]{0:T(512)S(1)} all-reduce(f32[512]{0:T(512)S(1)} %get-tuple-element.19), channel_id=1, replica_groups=mesh['section'=8,'replica'=64] {'replica'}, use_global_device_ids=true, to_apply=%region_3.0 | all-reduce | flops 512 | bytes 4096 | tf_op jit(solution)/shard_map/psum | solution.py:32
  205.1 0.5 copy.31
  205.6 0.2 reshape.26
  206.2 0.2 reshape.31
  206.5 4.6 select_reduce_fusion.5
  211.2 45.7 %all-gather.5 = f32[64,1,512]{2,1,0:T(1,128)S(1)} all-gather(f32[1,1,512]{2,1,0:T(1,128)S(1)} %bitcast.99), channel_id=3, replica_groups=mesh['section'=8,'replica'=64] {'replica'}, dimensions={0}, use_global_device_ids=true | all-gather | bytes 133120 | tf_op jit(solution)/shard_map/all_gather | solution.py:29
  257.0 0.2 select_reduce_fusion.4
  257.2 140.6 %psum.29 = f32[512]{0:T(512)S(1)} all-reduce(f32[512]{0:T(512)S(1)} %get-tuple-element.17), channel_id=1, replica_groups=mesh['section'=8,'replica'=64] {'replica'}, use_global_device_ids=true, to_apply=%region_7.0 | all-reduce | flops 512 | bytes 4096 | tf_op jit(solution)/shard_map/psum | solution.py:32
  397.8 0.5 copy.34
  398.3 0.2 reshape.35
  398.7 1.9 collective-permute-start
  400.8 7.7 collective-permute-done
  408.7 0.2 reshape.40
  409.1 4.7 select_reduce_fusion.3
  413.8 45.7 %all-gather.6 = f32[64,1,512]{2,1,0:T(1,128)S(1)} all-gather(f32[1,1,512]{2,1,0:T(1,128)S(1)} %bitcast.100), channel_id=4, replica_groups=mesh['section'=8,'replica'=64] {'replica'}, dimensions={0}, use_global_device_ids=true | all-gather | bytes 133120 | tf_op jit(solution)/shard_map/all_gather | solution.py:29
  459.6 0.2 select_reduce_fusion.2
  459.8 140.7 %psum.30 = f32[512]{0:T(512)S(1)} all-reduce(f32[512]{0:T(512)S(1)} %get-tuple-element.15), channel_id=1, replica_groups=mesh['section'=8,'replica'=64] {'replica'}, use_global_device_ids=true, to_apply=%region_11.12 | all-reduce | flops 512 | bytes 4096 | tf_op jit(solution)/shard_map/psum | solution.py:32
  600.5 0.5 copy.38
  601.0 0.2 reshape.44
  601.5 0.2 reshape.49
  601.9 4.7 select_reduce_fusion.1
  606.5 45.9 %all-gather.7 = f32[64,1,512]{2,1,0:T(1,128)S(1)} all-gather(f32[1,1,512]{2,1,0:T(1,128)S(1)} %bitcast.101), channel_id=5, replica_groups=mesh['section'=8,'replica'=64] {'replica'}, dimensions={0}, use_global_device_ids=true | all-gather | bytes 133120 | tf_op jit(solution)/shard_map/all_gather | solution.py:29
  652.5 0.2 select_reduce_fusion
  652.7 140.6 %psum.31 = f32[512]{0:T(512)S(1)} all-reduce(f32[512]{0:T(512)S(1)} %get-tuple-element.13), channel_id=1, replica_groups=mesh['section'=8,'replica'=64] {'replica'}, use_global_device_ids=true, to_apply=%region_15.16 | all-reduce | flops 512 | bytes 4096 | tf_op jit(solution)/shard_map/psum | solution.py:32
  793.4 0.5 copy.41
  794.4 1.7 copy.42
  (39 shorter events, 2.9 us)
Async XLA Ops:
  0.0 3.2 copy-start.1
  398.3 10.2 %copy-start = (bf16[1,2,14,14,512]{4,1,3,2,0:T(2,128)(2,1)S(1)}, bf16[1,2,14,14,512]{4,1,3,2,0:T(2,128)(2,1)}, u32[]{:S(2)}) copy-start(bf16[1,2,14,14,512]{4,1,3,2,0:T(2,128)(2,1)} %param.7) | copy-start | bytes 1204228
  398.7 9.8 %collective-permute-start = (bf16[2,14,14,512]{3,2,0,1:T(8,128)(2,1)S(1)}, bf16[2,14,14,512]{3,2,0,1:T(8,128)(2,1)S(1)}, u32[]{:S(2)}, u32[]{:S(2)}) collective-permute-start(bf16[2,14,14,512]{3,2,0,1:T(8,128)(2,1)S(1)} %maximum_convert_fusion.2), channel_id=1, source_target_pairs={{0,64},{64,128},{128,192},{192,256},{256,320},{320,384},{384,448},... | collective-permute-start | bytes 1204232 | tf_op jit(solution)/shard_map/ppermute | solution.py:13
